TPU v7x, 128 devices: a whole 4x4x4 slice. The times are simulated.
128 devices in a mesh: prow: 16 (over x, z_hi, core), pcol: 8 (over z_lo, y).
Axes of the slice: x: 4, y: 4, z: 4 (z_hi: 2, z_lo: 2; z = z_hi * 2 + z_lo), core: 2. Of those that a mesh axis runs over, the one named last changes fastest.
Arguments:
- inverse: bfloat16 [4, 8192, 8, 4096], P(None, 'prow', None, 'pcol'), may hold values from -6 to 6
- panel: bfloat16 [2, 4, 8192, 256], P(None, None, 'prow'), may hold values from -0.0625 to 0.0625
- structure: int32 [2, 16], replicated, may hold values from 0 to 63, as said below
- diag_inverse: float32 [2, 256, 256], replicated, may hold values from -6 to 6
Outputs:
- off_diag: bfloat16 [2, 4, 8192, 256], P(None, None, ('prow', 'pcol'))
- diag_block: float32 [2, 256, 256], replicated
Inputs may be any that keep to these rules, and one draw needn't show every extreme that they name: `structure`: each row lists 16 distinct block indices in increasing order, exactly one of them congruent to p modulo 16 for every p, and always includes the last ancestor block 63.
All inputs are finite; a program needn't handle non-finite values.
Results may differ from a plain program's by a relative error of at most 0.0022.
Values may be sent and summed in bfloat16 or wider, within the bound.
No kernel may reach another device: no remote copies, remote signals or barrier semaphores. Data moves between devices by JAX's collectives and lax.ppermute only.
A program may use at most 128 MiB of HBM per device.

v0:
```python
import jax
import jax.numpy as jnp
from jax import lax
from jax.sharding import PartitionSpec as P


def cut_along(array, dim, count):
    before, after = (array.shape[:dim], array.shape[dim + 1 :])
    return jnp.moveaxis(array.reshape(*before, count, -1, *after), dim, 0)


def sum_at_owner(array, axis, dim):
    tiles = cut_along(array, dim, lax.axis_size(axis))
    arrived = lax.all_to_all(tiles, axis, split_axis=0, concat_axis=0, tiled=True)
    return arrived.sum(axis=0)


def on_device(inverse, panel, structure, diag_inverse):
    prow_count = lax.axis_size("prow")
    pcol_count = lax.axis_size("pcol")
    prow_index = lax.axis_index("prow")
    pcol_index = lax.axis_index("pcol")
    rows_local, block_size, cols_local, _ = inverse.shape
    panel_width = panel.shape[3]
    total_blocks = rows_local * prow_count
    piece_rows = block_size // pcol_count
    owner_ratio = prow_count // pcol_count
    repeat_count = cols_local // owner_ratio
    positions = jnp.arange(total_blocks, dtype=jnp.int32)
    local_rows = jnp.arange(rows_local, dtype=jnp.int32)
    pieces = []
    products = []
    for supernode in range(structure.shape[0]):
        chosen = structure[supernode]
        selected = jnp.any(chosen[:, None] == positions[None, :], axis=0)
        own_rows = lax.dynamic_index_in_dim(
            selected.reshape(rows_local, prow_count), prow_index, 1, keepdims=False
        )
        own_cols = lax.dynamic_index_in_dim(
            selected.reshape(cols_local, pcol_count), pcol_index, 1, keepdims=False
        )
        local_panel = panel[supernode]
        row_pick = jnp.sum(jnp.where(own_rows, local_rows, 0))
        single = lax.dynamic_index_in_dim(local_panel, row_pick, 0, keepdims=False)
        gathered = lax.all_gather(single, "prow", axis=0, tiled=True)
        gathered = gathered.reshape(owner_ratio, pcol_count, block_size, panel_width)
        owner_blocks = lax.dynamic_index_in_dim(gathered, pcol_index, 1, keepdims=False)
        tiled = jnp.broadcast_to(
            owner_blocks[None], (repeat_count, owner_ratio, block_size, panel_width)
        )
        tiled = tiled.reshape(cols_local, block_size, panel_width)
        column_panel = tiled * own_cols.astype(jnp.bfloat16)[:, None, None]
        ranking = jnp.where(own_cols, 0, cols_local) + jnp.arange(cols_local, dtype=jnp.int32)
        column_order = jnp.argsort(ranking)
        live_count = jnp.sum(own_cols.astype(jnp.int32))

        def add_column(position_index, running):
            column = column_order[position_index]
            block_column = lax.dynamic_index_in_dim(inverse, column, 2, keepdims=False)
            factor = lax.dynamic_index_in_dim(column_panel, column, 0, keepdims=False)
            return running + jnp.einsum(
                "rab,bw->raw", block_column, factor, preferred_element_type=jnp.float32
            )

        starting = jnp.zeros((rows_local, block_size, panel_width), jnp.float32)
        partial_value = lax.fori_loop(0, live_count, add_column, starting)
        partial_value = -partial_value * own_rows.astype(jnp.float32)[:, None, None]
        summed = sum_at_owner(partial_value, "pcol", 1)
        rounded = summed.astype(jnp.bfloat16)
        pieces.append(rounded)
        factor_rows = lax.dynamic_slice_in_dim(local_panel, pcol_index * piece_rows, piece_rows, 1)
        products.append(
            jnp.einsum("raw,rav->wv", factor_rows, rounded, preferred_element_type=jnp.float32)
        )
    diagonal_terms = lax.psum(jnp.stack(products), ("prow", "pcol"))
    return (jnp.stack(pieces), diag_inverse - diagonal_terms)


def solution(mesh):
    placed = (P(None, "prow", None, "pcol"), P(None, None, "prow", None), P(), P())
    return jax.shard_map(
        on_device,
        mesh=mesh,
        in_specs=placed,
        out_specs=(P(None, None, ("prow", "pcol"), None), P()),
        check_vma=False,
    )
```

profile of v0, /device:TPU:1, one launch (start us, length us, event | category | flops | bytes accessed | tf_op | source)
XLA Modules:
  0.0 347.8 jit_solution(9517647593599522379)
XLA Ops:
  7.2 0.8 slice_bitcast_fusion.1
  10.6 1.7 fusion.30
  13.0 0.7 constant_dynamic-slice_fusion.3
  15.7 0.7 constant_dynamic-slice_fusion
  16.7 16.7 %copy.16 = bf16[4,512,8,512]{3,1,0,2:T(8,128)(2,1)} copy(bf16[4,512,8,512]{3,2,1,0:T(8,128)(2,1)} %param.8) | data formatting | bytes 33554432 | tf_op jit(solution)/shard_map/while | solution.py:66
  33.5 0.8 select_reduce_fusion.1
  34.3 1.0 sort.31
  35.3 0.8 select_reduce_fusion
  36.1 37.5 %all-gather.5.cloned.1.call-done = bf16[1,1,8192,256]{3,2,1,0:T(8,128)(2,1)} async-done(((bf16[1,1,512,256]{3,2,1,0:T(8,128)(2,1)}), bf16[1,1,8192,256]{3,2,1,0:T(8,128)(2,1)}) %all-gather.5.cloned.1.call-update) | async-done | bytes 4194320 | tf_op jit(solution)/shard_map/all_gather | solution.py:45
  73.6 1.1 dynamic-slice_bitcast_fusion.1
  74.7 1.6 bitcast_multiply_fusion.1
  76.4 11.7 %while.20 = (s32[]{:T(128)}, f32[4,512,256]{2,1,0:T(8,128)S(1)}, s32[]{:T(128)}, s32[8]{0:T(128)S(1)}, bf16[4,512,8,512]{3,1,0,2:T(8,128)(2,1)}, /*index=5*/bf16...) while((s32[]{:T(128)}, f32[4,512,256]{2,1,0:T(8,128)S(1)}, s32[]{:T(128)}, s32[8]{0:T(128)S(1)}, ...), condition=%wide.region_5.6_spmd, body=%wide.region_4.5_spmd.sunk | while | flops 537395200 | bytes 6554797 | solution.py:66
  79.6 2.3 fusion.41
  85.1 2.4 fusion.41
  88.4 1.5 copy.17
  89.9 4.3 %all-to-all-start = ((f32[8,4,64,256]{3,2,1,0:T(8,128)}), f32[8,4,64,256]{3,2,1,0:T(8,128)}, u32[]{:S(2)}, u32[]{:S(2)}) async-start(f32[8,4,64,256]{3,2,1,0:T(8,128)} %copy.17), calls=%async_computation | async-start | bytes 4194304 | tf_op jit(solution)/shard_map/all_to_all | solution.py:14
  94.4 1.0 sort.32
  95.5 45.2 %all-gather.7.cloned.1.call-done = bf16[1,1,8192,256]{3,2,1,0:T(8,128)(2,1)} async-done(((bf16[1,1,512,256]{3,2,1,0:T(8,128)(2,1)}), bf16[1,1,8192,256]{3,2,1,0:T(8,128)(2,1)}) %all-gather.7.cloned.1.call-update) | async-done | bytes 4194320 | tf_op jit(solution)/shard_map/all_gather | solution.py:45
  140.7 1.1 dynamic-slice_bitcast_fusion
  141.7 1.6 bitcast_multiply_fusion
  143.5 11.8 %while.21 = (s32[]{:T(128)}, f32[4,512,256]{2,1,0:T(8,128)S(1)}, s32[]{:T(128)}, s32[8]{0:T(128)S(1)}, bf16[4,512,8,512]{3,1,0,2:T(8,128)(2,1)}, /*index=5*/bf16...) while((s32[]{:T(128)}, f32[4,512,256]{2,1,0:T(8,128)S(1)}, s32[]{:T(128)}, s32[8]{0:T(128)S(1)}, ...), condition=%wide.region_12.13_spmd, body=%wide.region_11.12_spmd.sunk | while | flops 537395200 | bytes 6554797 | solution.py:66
  146.7 2.3 fusion.44
  152.3 2.3 fusion.44
  155.6 1.5 copy.19
  157.1 4.3 %all-to-all-start.1 = ((f32[8,4,64,256]{3,2,1,0:T(8,128)}), f32[8,4,64,256]{3,2,1,0:T(8,128)S(1)}, u32[]{:S(2)}, u32[]{:S(2)}) async-start(f32[8,4,64,256]{3,2,1,0:T(8,128)} %copy.19), calls=%async_computation.1 | async-start | bytes 4194304 | tf_op jit(solution)/shard_map/all_to_all | solution.py:14
  161.4 1.7 reduce_sum.56
  163.1 1.8 convolution_bitcast_fusion.1
  165.0 23.5 %all-to-all-done.1 = f32[8,4,64,256]{3,2,1,0:T(8,128)S(1)} async-done(((f32[8,4,64,256]{3,2,1,0:T(8,128)}), f32[8,4,64,256]{3,2,1,0:T(8,128)S(1)}, u32[]{:S(2)}, u32[]{:S(2)}) %all-to-all-start.1) | async-done | bytes 2097184 | tf_op jit(solution)/shard_map/all_to_all | solution.py:14
  188.8 1.8 pad_maximum_fusion
  190.6 0.7 pad_maximum_fusion.1
  191.4 148.0 %all-reduce.2.cloned.1.call-done = f32[2,256,256]{2,1,0:T(8,128)} async-done(((f32[2,256,256]{2,1,0:T(8,128)}), f32[2,256,256]{2,1,0:T(8,128)}) %all-reduce.2.cloned.1.call-update) | async-done | bytes 524304 | tf_op jit(solution)/shard_map/psum | solution.py:75
  339.4 1.9 sub.3
  (38 shorter events, 5.7 us)
Async XLA Ops:
  7.2 66.4 %all-gather.5.cloned.1.call-start = ((), (), s32[]{:S(2)}) async-start(), calls=%async_computation.3 | async-start | bytes 4456448 | tf_op jit(solution)/shard_map/all_gather | solution.py:45
  12.3 21.0 %copy-start = (bf16[1,4,512,256]{3,2,1,0:T(8,128)(2,1)}, bf16[1,4,512,256]{3,2,1,0:T(8,128)(2,1)S(1)}, u32[]{:S(2)}) copy-start(bf16[1,4,512,256]{3,2,1,0:T(8,128)(2,1)S(1)} %get-tuple-element.162) | copy-start | bytes 3145732
  13.7 126.9 %all-gather.7.cloned.1.call-start = ((), (), s32[]{:S(2)}) async-start(), calls=%async_computation.4 | async-start | bytes 4456448 | tf_op jit(solution)/shard_map/all_gather | solution.py:45
  89.9 67.2 %all-to-all-start = ((f32[8,4,64,256]{3,2,1,0:T(8,128)}), f32[8,4,64,256]{3,2,1,0:T(8,128)}, u32[]{:S(2)}, u32[]{:S(2)}) async-start(f32[8,4,64,256]{3,2,1,0:T(8,128)} %copy.17), calls=%async_computation | async-start | bytes 4194304 | tf_op jit(solution)/shard_map/all_to_all | solution.py:14
  157.1 31.4 %all-to-all-start.1 = ((f32[8,4,64,256]{3,2,1,0:T(8,128)}), f32[8,4,64,256]{3,2,1,0:T(8,128)S(1)}, u32[]{:S(2)}, u32[]{:S(2)}) async-start(f32[8,4,64,256]{3,2,1,0:T(8,128)} %copy.19), calls=%async_computation.1 | async-start | bytes 4194304 | tf_op jit(solution)/shard_map/all_to_all | solution.py:14
  161.4 178.0 %all-reduce.2.cloned.1.call-start = ((), (), s32[]{:S(2)}) async-start(), calls=%async_computation.2 | async-start | bytes 1048576 | tf_op jit(solution)/shard_map/psum | solution.py:75
  188.6 150.8 %copy-start.1 = (f32[2,256,256]{2,1,0:T(8,128)S(1)}, f32[2,256,256]{2,1,0:T(8,128)}, u32[]{:S(2)}) copy-start(f32[2,256,256]{2,1,0:T(8,128)} %param.11) | copy-start | bytes 1572868
Sparse Core Ops, SparseCore 0:
  13.9 59.6 all-gather.4
  76.6 64.0 all-gather.6
  190.8 148.5 all-reduce.1
where the time goes:
time: 349 us; the launch traced here: 348 us
  waiting for transfers between devices  254 us (73%)
  local copies, waits for them, and re-layouts  29.1 us (8%)
  between operations  17.8 us (5%)
  other arithmetic  14.8 us (4%)
  loops' own time  11.8 us (3%)
  matrix products  11.4 us (3%)
  starting transfers between devices  8.73 us (3%)
    psum x1, waiting for transfers between devices, on_device(): diagonal_terms = lax.psum(jnp.stack(products), ('prow', 'pcol'))  148 us
    all_gather x2, waiting for transfers between devices, on_device(): gathered = lax.all_gather(single, 'prow', axis=0, tiled=True)  82.7 us
    all_to_all x2, waiting for transfers between devices, sum_at_owner(): lax.all_to_all(tiles, axis, split_axis=0, concat_axis=0, tiled=True)  23.5 us
    while x1, local copies, waits for them, and re-layouts, on_device(): partial_value = lax.fori_loop(0, live_count, add_column, starting)  16.7 us
    another operation x2, loops' own time, on_device(): partial_value = lax.fori_loop(0, live_count, add_column, starting)  11.8 us
    dot_general x4, matrix products, add_column(): jnp.einsum('rab,bw->raw', block_column, factor, preferred_element_type=jn...  9.32 us
    all_to_all x2, starting transfers between devices, sum_at_owner(): lax.all_to_all(tiles, axis, split_axis=0, concat_axis=0, tiled=True)  8.61 us
  transfers between devices with their start and end apart: 5, of which 4 were waited for; matrix products, arithmetic and copies ran while one was open for 13% of the time, Pallas kernels for 0%

commit v1 on v0

--- a/solution.py
+++ b/solution.py
@@ -72,7 +72,11 @@
         products.append(
             jnp.einsum("raw,rav->wv", factor_rows, rounded, preferred_element_type=jnp.float32)
         )
-    diagonal_terms = lax.psum(jnp.stack(products), ("prow", "pcol"))
+
+    def scenes_form(field):
+        return lax.all_gather(field, axis_name=("prow", "pcol")).sum(axis=0)
+
+    diagonal_terms = scenes_form(jnp.stack(products))
     return (jnp.stack(pieces), diag_inverse - diagonal_terms)
 
 

time: 349 us -> 613 us (1.76)
  waiting for transfers between devices: 254 us -> 498 us
  other arithmetic: 14.8 us -> 34.7 us
    all_gather x0 -> x1, waiting for transfers between devices: none -> 392 us  [scenes_form(): return lax.all_gather(field, axis_name=('prow', 'pcol')).sum(axis=0)]
    psum x1 -> x0, waiting for transfers between devices: 148 us -> none  [on_device(): diagonal_terms = lax.psum(jnp.stack(products), ('prow', 'pcol'))]
    reduce_sum x0 -> x1, other arithmetic: none -> 20.9 us  [scenes_form(): return lax.all_gather(field, axis_name=('prow', 'pcol')).sum(axis=0)]
  transfers between devices with their start and end apart: 5 -> 5, of which waited for: 4 -> 4; matrix products, arithmetic and copies ran while one was open for 13% -> 8% of each run, Pallas kernels for 0% -> 0%
where the time goes in v1:
time: 613 us; the launch traced here: 612 us
  waiting for transfers between devices  498 us (81%)
  other arithmetic  34.7 us (6%)
  local copies, waits for them, and re-layouts  29.1 us (5%)
  between operations  17.8 us (3%)
  loops' own time  11.8 us (2%)
  matrix products  11.4 us (2%)
  starting transfers between devices  8.73 us (1%)
    all_gather x1, waiting for transfers between devices, scenes_form(): return lax.all_gather(field, axis_name=('prow', 'pcol')).sum(axis=0)  392 us
    all_gather x2, waiting for transfers between devices, on_device(): gathered = lax.all_gather(single, 'prow', axis=0, tiled=True)  82.7 us
    all_to_all x2, waiting for transfers between devices, sum_at_owner(): lax.all_to_all(tiles, axis, split_axis=0, concat_axis=0, tiled=True)  23.5 us
    reduce_sum x1, other arithmetic, scenes_form(): return lax.all_gather(field, axis_name=('prow', 'pcol')).sum(axis=0)  20.9 us
    while x1, local copies, waits for them, and re-layouts, on_device(): partial_value = lax.fori_loop(0, live_count, add_column, starting)  16.7 us
  transfers between devices with their start and end apart: 5, of which 4 were waited for; matrix products, arithmetic and copies ran while one was open for 8% of the time, Pallas kernels for 0%

profile of v1, /device:TPU:1, one launch (start us, length us, event | category | flops | bytes accessed | tf_op | source)
XLA Modules:
  0.0 611.9 jit_solution(17691803305578428339)
XLA Ops:
  7.2 0.8 slice_bitcast_fusion.1
  10.6 1.7 fusion.30
  13.0 0.7 constant_dynamic-slice_fusion.3
  16.7 16.7 %copy.16 = bf16[4,512,8,512]{3,1,0,2:T(8,128)(2,1)} copy(bf16[4,512,8,512]{3,2,1,0:T(8,128)(2,1)} %param.8) | data formatting | bytes 33554432 | tf_op jit(solution)/shard_map/while | solution.py:66
  33.5 0.8 select_reduce_fusion.1
  34.3 1.0 sort.31
  35.3 0.8 select_reduce_fusion
  36.1 37.5 %all-gather.7.cloned.1.call-done = bf16[1,1,8192,256]{3,2,1,0:T(8,128)(2,1)} async-done(((bf16[1,1,512,256]{3,2,1,0:T(8,128)(2,1)}), bf16[1,1,8192,256]{3,2,1,0:T(8,128)(2,1)}) %all-gather.7.cloned.1.call-update) | async-done | bytes 4194320 | tf_op jit(solution)/shard_map/all_gather | solution.py:45
  73.6 1.1 dynamic-slice_bitcast_fusion.1
  74.7 1.6 bitcast_multiply_fusion.1
  76.4 11.7 %while.20 = (s32[]{:T(128)}, f32[4,512,256]{2,1,0:T(8,128)S(1)}, s32[]{:T(128)}, s32[8]{0:T(128)S(1)}, bf16[4,512,8,512]{3,1,0,2:T(8,128)(2,1)}, /*index=5*/bf16...) while((s32[]{:T(128)}, f32[4,512,256]{2,1,0:T(8,128)S(1)}, s32[]{:T(128)}, s32[8]{0:T(128)S(1)}, ...), condition=%wide.region_5.6_spmd, body=%wide.region_4.5_spmd.sunk | while | flops 537395200 | bytes 6554797 | solution.py:66
  79.6 2.3 fusion.41
  85.1 2.4 fusion.41
  88.4 1.5 copy.17
  89.9 4.3 all-to-all-start
  94.4 1.0 sort.32
  95.5 45.2 %all-gather.9.cloned.1.call-done = bf16[1,1,8192,256]{3,2,1,0:T(8,128)(2,1)} async-done(((bf16[1,1,512,256]{3,2,1,0:T(8,128)(2,1)}), bf16[1,1,8192,256]{3,2,1,0:T(8,128)(2,1)}) %all-gather.9.cloned.1.call-update) | async-done | bytes 4194320 | tf_op jit(solution)/shard_map/all_gather | solution.py:45
  140.7 1.1 dynamic-slice_bitcast_fusion
  141.7 1.6 bitcast_multiply_fusion
  143.5 11.8 %while.21 = (s32[]{:T(128)}, f32[4,512,256]{2,1,0:T(8,128)S(1)}, s32[]{:T(128)}, s32[8]{0:T(128)S(1)}, bf16[4,512,8,512]{3,1,0,2:T(8,128)(2,1)}, /*index=5*/bf16...) while((s32[]{:T(128)}, f32[4,512,256]{2,1,0:T(8,128)S(1)}, s32[]{:T(128)}, s32[8]{0:T(128)S(1)}, ...), condition=%wide.region_12.13_spmd, body=%wide.region_11.12_spmd.sunk | while | flops 537395200 | bytes 6554797 | solution.py:66
  146.7 2.3 fusion.44
  152.3 2.3 fusion.44
  155.6 1.5 copy.19
  157.1 4.3 all-to-all-start.1
  161.4 1.7 reduce_sum.65
  163.1 1.8 convolution_bitcast_fusion.1
  165.0 23.5 %all-to-all-done.1 = f32[8,4,64,256]{3,2,1,0:T(8,128)S(1)} async-done(((f32[8,4,64,256]{3,2,1,0:T(8,128)}), f32[8,4,64,256]{3,2,1,0:T(8,128)S(1)}, u32[]{:S(2)}, u32[]{:S(2)}) %all-to-all-start.1) | async-done | bytes 2097184 | tf_op jit(solution)/shard_map/all_to_all | solution.py:14
  188.8 1.8 pad_maximum_fusion
  190.6 0.7 pad_maximum_fusion.1
  191.4 392.2 %all-gather.11.cloned.1.call-done = f32[256,256,256]{2,1,0:T(8,128)} async-done(((f32[2,256,256]{2,1,0:T(8,128)}), f32[256,256,256]{2,1,0:T(8,128)}) %all-gather.11.cloned.1.call-update) | async-done | bytes 67108880 | tf_op jit(solution)/shard_map/all_gather | solution.py:77
  583.6 20.9 %reduce_sum.69 = f32[2,256,256]{2,1,0:T(8,128)S(1)} reduce(f32[128,2,256,256]{3,2,1,0:T(8,128)} %bitcast.28, f32[]{:T(128)} %constant.66.clone.1), dimensions={0}, to_apply=%region_14.15 | reduce | flops 16646144 | bytes 67633152 | tf_op jit(solution)/shard_map/reduce_sum | solution.py:77
  604.5 0.9 sub.3
  (39 shorter events, 6.4 us)
Async XLA Ops:
  7.2 66.4 %all-gather.7.cloned.1.call-start = ((), (), s32[]{:S(2)}) async-start(), calls=%async_computation.2 | async-start | bytes 4456448 | tf_op jit(solution)/shard_map/all_gather | solution.py:45
  12.3 21.0 %copy-start = (bf16[1,4,512,256]{3,2,1,0:T(8,128)(2,1)}, bf16[1,4,512,256]{3,2,1,0:T(8,128)(2,1)S(1)}, u32[]{:S(2)}) copy-start(bf16[1,4,512,256]{3,2,1,0:T(8,128)(2,1)S(1)} %get-tuple-element.162) | copy-start | bytes 3145732
  13.7 126.9 %all-gather.9.cloned.1.call-start = ((), (), s32[]{:S(2)}) async-start(), calls=%async_computation.3 | async-start | bytes 4456448 | tf_op jit(solution)/shard_map/all_gather | solution.py:45
  89.9 67.2 %all-to-all-start = ((f32[8,4,64,256]{3,2,1,0:T(8,128)}), f32[8,4,64,256]{3,2,1,0:T(8,128)}, u32[]{:S(2)}, u32[]{:S(2)}) async-start(f32[8,4,64,256]{3,2,1,0:T(8,128)} %copy.17), calls=%async_computation | async-start | bytes 4194304 | tf_op jit(solution)/shard_map/all_to_all | solution.py:14
  157.1 31.4 %all-to-all-start.1 = ((f32[8,4,64,256]{3,2,1,0:T(8,128)}), f32[8,4,64,256]{3,2,1,0:T(8,128)S(1)}, u32[]{:S(2)}, u32[]{:S(2)}) async-start(f32[8,4,64,256]{3,2,1,0:T(8,128)} %copy.19), calls=%async_computation.1 | async-start | bytes 4194304 | tf_op jit(solution)/shard_map/all_to_all | solution.py:14
  161.4 422.2 %all-gather.11.cloned.1.call-start = ((), (), s32[]{:S(2)}) async-start(), calls=%async_computation.4 | async-start | bytes 67633152 | tf_op jit(solution)/shard_map/all_gather | solution.py:77
  583.6 20.9 %copy-start.1 = (f32[2,256,256]{2,1,0:T(8,128)S(1)}, f32[2,256,256]{2,1,0:T(8,128)}, u32[]{:S(2)}) copy-start(f32[2,256,256]{2,1,0:T(8,128)} %param.11) | copy-start | bytes 1572868
Sparse Core Ops, SparseCore 0:
  13.9 59.6 all-gather.6
  76.6 64.0 all-gather.8
  190.7 392.7 all-gather.10
